TPU v7x, 32 devices: a whole 2x2x4 slice. The times are simulated.
32 devices in a mesh: space: 4 (over y, core), mode: 8 (over z, x).
Axes of the slice: x: 2, y: 2, z: 4, core: 2. Of those that a mesh axis runs over, the one named last changes fastest.
Arguments:
- intensity: float32 [1024, 8, 64, 256], P('mode', None, 'space'), may hold values from 0.1 to 2
- dir_cos: float32 [3, 32], replicated, may hold values from -1 to 1, as said below
- velocity: float32 [32], replicated, may hold values from 0.2 to 1
- rate: float32 [32], replicated, may hold values from 0.05 to 2
- spectrum: float32 [32], replicated, may hold values from 0.2 to 2
- weight: float32 [32], replicated, may hold values from 0.25 to 1.75
- heat: float32 [64, 256], P('space'), may hold values from 0.5 to 4
- rough_cells: int32 [4096], P('space'), may hold values from 0 to 4095, as said below
- rough_count: int32 [4], P('space'), may hold values from 256 to 1024, as said below
- rough_map: int32 [4096, 16], P('space'), may hold values from 0 to 15
Outputs:
- intensity_new: float32 [1024, 8, 64, 256], P('mode', None, 'space')
- energy_new: float32 [8, 64, 256], P(None, 'space')
Inputs may be any that keep to these rules, and one draw needn't show every extreme that they name: `dir_cos`: even directions have a positive third cosine, and direction 2k+1 equals direction 2k with the third cosine negated; every direction has a third cosine of magnitude 0.3 or more. `rough_cells`: the entries of one index of space are distinct. `rough_count`: some index of space has all 1024 slots live.
All inputs are finite; a program needn't handle non-finite values.
Results may differ from a plain program's by a relative error of at most 0.0015.
Values sent between devices are 32-bit elements; how exact they have to be, the bound alone decides.
A program may use at most 128 MiB of HBM per device.

v0:
```python
import jax
import jax.numpy as jnp
from jax import lax
from jax.sharding import PartitionSpec as P

PAIRS = 1024


def extended(block, sides, width):
    for axis, dim in sides:
        count = lax.axis_size(axis)
        forward = [(i, i + 1) for i in range(count - 1)]
        backward = [(target, source) for source, target in forward]
        low = lax.ppermute(
            lax.slice_in_dim(block, block.shape[dim] - width, None, axis=dim), axis, forward
        )
        high = lax.ppermute(lax.slice_in_dim(block, 0, width, axis=dim), axis, backward)
        block = jnp.concatenate([low, block, high], axis=dim)
    return block


def squash(energy):
    return energy / (1.0 + 0.3 * jnp.abs(energy))


def per_device(
    intensity, dir_cos, velocity, rate, spectrum, weight, heat, rough_cells, rough_count, rough_map
):
    pairs_local = intensity.shape[0]
    modes = velocity.shape[0]
    planes_count, rows, width = (intensity.shape[1], intensity.shape[2], intensity.shape[3])
    dirs_local = pairs_local // modes
    half = dirs_local // 2
    position = lax.axis_index("mode")
    cos_local = lax.dynamic_slice_in_dim(dir_cos, position * dirs_local, dirs_local, 1)
    weight_local = lax.dynamic_slice_in_dim(weight, position * dirs_local, dirs_local, 0)
    field = intensity.reshape(dirs_local, modes, planes_count, rows, width)
    partial_value = jnp.einsum("s,smzxy->zxy", weight_local, field)
    energy = lax.psum(partial_value, "mode") / PAIRS
    equil = squash(energy)
    padded = extended(field, (("space", 3),), 1)
    ox = cos_local[0][:, None, None, None, None]
    oy = cos_local[1][:, None, None, None, None]
    speed = velocity[None, :, None, None, None]
    pady = jnp.pad(field, ((0, 0), (0, 0), (0, 0), (0, 0), (1, 1)))
    along = jnp.maximum(ox, 0.0) * (field - padded[:, :, :, :-2]) + jnp.minimum(ox, 0.0) * (
        padded[:, :, :, 2:] - field
    )
    across = jnp.maximum(oy, 0.0) * (field - pady[..., :-2]) + jnp.minimum(oy, 0.0) * (
        pady[..., 2:] - field
    )
    source = (rate * spectrum)[:, None, None, None] * equil[None]
    rhs = field + source[None] - speed * (along + across)
    diag = 1.0 + rate
    couple = velocity[None, :] * jnp.abs(cos_local[2])[:, None]
    cdown = couple[1::2][:, :, None, None]
    adown = diag[None, :, None, None] + cdown
    down_rhs = rhs[1::2]
    carry = spectrum[None, :, None, None] * heat[None, None]
    planes = [None] * planes_count
    for level in reversed(range(planes_count)):
        carry = (down_rhs[:, :, level] + cdown * carry) / adown
        planes[level] = carry
    down_new = jnp.stack(planes, axis=2)
    bottom = down_new[:, :, 0].reshape(half, modes, rows * width)
    slots = rough_cells.shape[0]
    live = jnp.arange(slots, dtype=jnp.int32) < rough_count[0]
    everything = lax.all_gather(bottom, "mode", axis=0, tiled=True)
    values = everything[:, :, rough_cells]
    targets = lax.dynamic_slice_in_dim(rough_map, position * half, half, 1)
    picked = jnp.take_along_axis(values.transpose(2, 0, 1), targets[:, :, None], axis=1).transpose(
        1, 2, 0
    )
    current = bottom[:, :, rough_cells]
    inflow = 0.9 * bottom.at[:, :, rough_cells].set(jnp.where(live[None, None, :], picked, current))
    carry = inflow.reshape(half, modes, rows, width)
    cup = couple[0::2][:, :, None, None]
    aup = diag[None, :, None, None] + cup
    up_rhs = rhs[0::2]
    planes = []
    for level in range(planes_count):
        carry = (up_rhs[:, :, level] + cup * carry) / aup
        planes.append(carry)
    up_new = jnp.stack(planes, axis=2)
    fresh = jnp.stack([up_new, down_new], axis=1).reshape(
        dirs_local, modes, planes_count, rows, width
    )
    energy_new = lax.psum(jnp.einsum("s,smzxy->zxy", weight_local, fresh), "mode") / PAIRS
    return (fresh.reshape(pairs_local, planes_count, rows, width), energy_new)


def solution(mesh):
    in_specs = (
        P("mode", None, "space", None),
        P(),
        P(),
        P(),
        P(),
        P(),
        P("space", None),
        P("space"),
        P("space"),
        P("space", None),
    )
    out_specs = (P("mode", None, "space", None), P(None, "space", None))
    return jax.shard_map(
        per_device, mesh=mesh, in_specs=in_specs, out_specs=out_specs, check_vma=False
    )
```

profile of v0, /device:TPU:0, one launch (start us, length us, event | category | flops | bytes accessed | tf_op | source)
XLA Modules:
  0.0 554.9 jit_solution(16689023233069573652)
XLA Ops:
  7.2 7.9 %bitcast_reduce_fusion = bf16[4,8,16,256]{3,2,1,0:T(8,128)(2,1)S(1)} fusion(f32[128,8,16,256]{3,2,1,0:T(8,128)} %param.10), kind=kLoop, calls=%fused_computation.96 | loop fusion | flops 4063232 | bytes 17039360 | tf_op jit(solution)/shard_map/s,smzxy->zxy/reduce_sum | solution.py:38
  15.2 0.4 fusion.23
  15.5 0.7 copy.266
  16.3 8.0 %fusion.37 = (f32[4,32,8,1,256]{4,3,2,1,0:T(1,128)S(1)}, f32[4,32,8,1,256]{4,3,2,1,0:T(1,128)S(1)}) fusion(f32[4,32,8,16,256]{4,3,2,1,0:T(8,128)} %bitcast.67), kind=kLoop, calls=%fused_computation.99 | loop fusion | bytes 4194304 | tf_op jit(solution)/shard_map/slice | solution.py:15
  24.4 2.5 collective-permute-start
  26.9 1.0 copy.238
  27.9 1.5 collective-permute-start.1
  29.4 0.1 constant_dynamic-slice_fusion
  29.5 0.1 broadcast_multiply_fusion.5
  29.6 0.9 broadcast_multiply_fusion.3
  30.5 0.1 broadcast_multiply_fusion.2
  30.6 59.0 %all-reduce.4.cloned.1.call-done = f32[8,16,256]{2,1,0:T(8,128)} async-done(((f32[8,16,256]{2,1,0:T(8,128)}), f32[8,16,256]{2,1,0:T(8,128)}) %all-reduce.4.cloned.1.call-update) | async-done | bytes 131088 | tf_op jit(solution)/shard_map/psum | solution.py:39
  89.6 0.9 add_divide_fusion.8
  90.5 0.6 broadcast_multiply_fusion.1
  91.2 1.1 copy.237
  92.3 2.3 copy.239
  94.6 34.3 %fusion.5 = f32[4,32,8,16,256]{4,3,2,1,0:T(8,128)} fusion(f32[4,32,8,16,256]{4,3,2,1,0:T(8,128)} %bitcast.68, f32[4,32,8,1,256]{4,3,2,1,0:T(1,128)S(1)} %copy.239, f32[4,32,8,1,256]{4,3,2,1,0:T(1,128)S(1)} %copy.237, f32[4]{0:T(128)S(1)} %get-tuple-element.31, f32[4]{0:T(128)S(1)} %get-tuple-element.33, f32[4]{0:T(128)S(1)} %get-tuple-element.30, ...), kind=kLoop, calls=%fused_computation.11 | loop fusion | flops 67108864 | bytes 39846080 | tf_op jit(solution)/shard_map/sub | solution.py:53
  128.9 9.2 %fusion.36 = (f32[2,32,8,16,256]{4,3,2,1,0:T(8,128)}, f32[2,32,8,16,256]{4,3,2,1,0:T(8,128)S(1)}) fusion(f32[4,32,8,16,256]{4,3,2,1,0:T(8,128)} %fusion.5), kind=kLoop, calls=%fused_computation.98 | loop fusion | bytes 33554432 | tf_op jit(solution)/shard_map/slice | solution.py:79
  138.1 1.1 divide_dynamic-update-slice_fusion
  139.2 0.2 constant_dynamic-update-slice_fusion.12
  139.5 0.2 constant_dynamic-update-slice_fusion.10
  139.8 0.2 constant_dynamic-update-slice_fusion.8
  140.1 3.0 fusion.38
  143.2 3.4 copy-done.2
  146.6 2.5 squeeze.36
  149.0 2.4 squeeze.37
  151.4 2.4 squeeze.38
  153.8 2.4 squeeze.39
  156.2 2.4 squeeze.40
  158.6 1.1 squeeze.41
  159.8 0.2 squeeze.42
  160.0 0.2 squeeze.43
  160.2 4.9 add_divide_fusion.7
  165.0 0.3 all-reduce.6.cloned.1.call-start
  165.3 0.8 bitcast_or_fusion
  166.1 0.2 copy.242
  166.3 0.3 reshape.137
  166.6 0.8 and_bitcast_fusion
  167.4 0.3 copy.240
  168.4 5.9 %copy.244 = f32[2,32,4096]{1,0,2:T(2,128)} copy(f32[2,32,4096]{2,1,0:T(8,128)} %add_divide_fusion.7) | data formatting | bytes 2097152 | tf_op jit(solution)/shard_map/div | solution.py:62
  174.3 5.7 %gather_fusion.1 = f32[1024,2,32]{2,1,0:T(2,128)S(1)} fusion(f32[2,32,4096]{1,0,2:T(2,128)} %copy.244, s32[1024]{0:T(1024)S(1)} %get-tuple-element.27), kind=kCustom, calls=%fused_computation.1 | custom fusion | bytes 528384 | tf_op jit(solution)/shard_map/gather | solution.py:74
  180.0 108.7 %all-gather.2.cloned.1.call-done = f32[16,32,4096]{2,1,0:T(8,128)} async-done(((f32[2,32,4096]{2,1,0:T(8,128)}), f32[16,32,4096]{2,1,0:T(8,128)}) %all-gather.2.cloned.1.call-update) | async-done | bytes 8388624 | tf_op jit(solution)/shard_map/all_gather | solution.py:68
  288.8 23.2 %copy.241 = f32[16,32,4096]{1,0,2:T(8,128)} copy(f32[16,32,4096]{2,1,0:T(8,128)} %all-gather.2.cloned.1.call-done) | data formatting | bytes 16777216 | tf_op jit(solution)/shard_map/all_gather | solution.py:68
  312.0 19.9 %gather_fusion = f32[1024,16,32]{2,1,0:T(8,128)} fusion(f32[16,32,4096]{1,0,2:T(8,128)} %copy.241, s32[1024]{0:T(1024)S(1)} %get-tuple-element.27), kind=kCustom, calls=%fused_computation | custom fusion | bytes 4198400 | tf_op jit(solution)/shard_map/gather | solution.py:69
  331.9 20.6 %gather_fusion.2 = f32[2048,32]{1,0:T(8,128)S(1)} fusion(f32[1024,16,32]{2,1,0:T(8,128)} %gather_fusion, s32[2048]{0:T(1024)S(1)} %reshape.137), kind=kCustom, calls=%fused_computation.2 | custom fusion | bytes 540672 | tf_op jit(solution)/shard_map/jit(take_along_axis)/gather | solution.py:71
  352.5 3.9 fusion.22
  356.4 93.8 %scatter_fusion = f32[2,32,4096]{1,0,2:T(2,128)} fusion(f32[2,32,4096]{1,0,2:T(2,128)} %copy.244, s32[1024]{0:T(1024)S(1)} %get-tuple-element.28, f32[1024,2,32]{2,1,0:T(2,128)S(1)} %fusion.22), kind=kCustom, calls=%fused_computation.3 | custom fusion | bytes 790528 | tf_op jit(solution)/shard_map/scatter | solution.py:75
  450.2 5.8 %broadcast_multiply_fusion = f32[2,32,4096]{1,0,2:T(2,128)} fusion(f32[2,32,4096]{1,0,2:T(2,128)} %scatter_fusion), kind=kLoop, calls=%fused_computation.22 | loop fusion | flops 262144 | bytes 2097152 | tf_op jit(solution)/shard_map/mul | solution.py:75
  456.0 3.6 copy.254
  459.6 1.6 constant_dynamic-update-slice_fusion.6
  461.3 1.9 constant_dynamic-update-slice_fusion.5
  463.2 1.6 constant_dynamic-update-slice_fusion.4
  464.8 1.9 constant_dynamic-update-slice_fusion.3
  466.7 0.2 constant_dynamic-update-slice_fusion.2
  467.0 0.3 constant_dynamic-update-slice_fusion.1
  467.3 0.2 constant_dynamic-update-slice_fusion
  467.5 0.3 fusion.14
  467.8 1.1 slice-done.2
  468.9 1.3 slice-done.3
  470.2 6.9 %fusion.32 = (bf16[2,2,8,16,256]{4,3,2,1,0:T(8,128)(2,1)S(1)}, f32[2,2,32,8,16,256]{5,4,3,2,1,0:T(8,128)}) fusion(f32[2,1,32,8,16,256]{5,4,3,2,1,0:T(8,128)S(1)} %bitcast.76, f32[2,1,32,8,16,256]{5,4,3,2,1,0:T(8,128)S(1)} %bitcast.73), kind=kLoop, calls=%fused_computation.97 | loop fusion | flops 8257536 | bytes 33816576 | tf_op jit(solution)/shard_map/s,smzxy->zxy/reduce_sum | solution.py:88
  477.1 0.4 fusion.25
  477.5 0.7 copy.265
  478.1 68.6 %all-reduce.6.cloned.1.call-done = f32[8,16,256]{2,1,0:T(8,128)} async-done(((f32[8,16,256]{2,1,0:T(8,128)}), f32[8,16,256]{2,1,0:T(8,128)}) %all-reduce.6.cloned.1.call-update) | async-done | bytes 131088 | tf_op jit(solution)/shard_map/psum | solution.py:88
  546.8 1.6 broadcast_multiply_fusion.4
  (46 shorter events, 0.6 us)
Async XLA Ops:
  7.2 22.2 %copy-start = (f32[3,32]{1,0:T(4,128)S(1)}, f32[3,32]{1,0:T(4,128)}, u32[]{:S(2)}) copy-start(f32[3,32]{1,0:T(4,128)} %param.11) | copy-start | bytes 1156
  7.2 82.4 %all-reduce.4.cloned.1.call-start = ((), (), s32[]{:S(2)}) async-start(), calls=%async_computation | async-start | bytes 262144 | tf_op jit(solution)/shard_map/psum | solution.py:39
  7.2 7.9 %copy-start.9 = (f32[32]{0:T(128)S(1)}, f32[32]{0:T(128)}, u32[]{:S(2)}) copy-start(f32[32]{0:T(128)} %param.15) | copy-start | bytes 388
  15.1 14.4 %copy-start.4 = (f32[16,256]{1,0:T(8,128)S(1)}, f32[16,256]{1,0:T(8,128)}, u32[]{:S(2)}) copy-start(f32[16,256]{1,0:T(8,128)} %param.16) | copy-start | bytes 49156
  15.1 14.4 %copy-start.7 = (f32[32]{0:T(128)S(1)}, f32[32]{0:T(128)}, u32[]{:S(2)}) copy-start(f32[32]{0:T(128)} %param.12) | copy-start | bytes 388
  15.1 14.4 %copy-start.5 = (f32[32]{0:T(128)S(1)}, f32[32]{0:T(128)}, u32[]{:S(2)}) copy-start(f32[32]{0:T(128)} %param.14) | copy-start | bytes 388
  15.1 15.3 %copy-start.8 = (f32[32]{0:T(128)S(1)}, f32[32]{0:T(128)}, u32[]{:S(2)}) copy-start(f32[32]{0:T(128)} %param.13) | copy-start | bytes 388
  16.2 272.6 %all-gather.2.cloned.1.call-start = ((), (), s32[]{:S(2)}) async-start(), calls=%async_computation.1 | async-start | bytes 9437184 | tf_op jit(solution)/shard_map/all_gather | solution.py:68
  24.4 66.8 %collective-permute-start = (f32[4,32,8,1,256]{4,2,3,1,0:T(8,128)S(1)}, f32[4,32,8,1,256]{4,2,3,1,0:T(8,128)S(1)}, u32[]{:S(2)}, u32[]{:S(2)}) collective-permute-start(f32[4,32,8,1,256]{4,2,3,1,0:T(8,128)S(1)} %copy.236), channel_id=1, source_target_pairs={{0,8},{8,16},{16,24},{1,9},{9,17},{17,25},{2,10},{10,18},{18,26},{... | collective-permute-start | bytes 3145736 | tf_op jit(solution)/shard_map/ppermute | solution.py:14
  27.9 64.4 %collective-permute-start.1 = (f32[4,32,8,1,256]{4,2,3,1,0:T(8,128)}, f32[4,32,8,1,256]{4,2,3,1,0:T(8,128)}, u32[]{:S(2)}, u32[]{:S(2)}) collective-permute-start(f32[4,32,8,1,256]{4,2,3,1,0:T(8,128)} %copy.238), channel_id=1, source_target_pairs={{8,0},{16,8},{24,16},{9,1},{17,9},{25,17},{10,2},{18,10},{26,18},{... | collective-permute-start | bytes 3145736 | tf_op jit(solution)/shard_map/ppermute | solution.py:17
  143.2 3.4 copy-start.2
  146.5 12.1 %copy-start.3 = (f32[2,32,1,16,256]{4,3,2,1,0:T(8,128)S(1)}, f32[2,32,1,16,256]{4,3,2,1,0:T(8,128)}, u32[]{:S(2)}) copy-start(f32[2,32,1,16,256]{4,3,2,1,0:T(8,128)} %get-tuple-element.21) | copy-start | bytes 3145732
  159.8 8.6 %copy-start.6 = (s32[1024]{0:T(1024)S(1)}, s32[1024]{0:T(1024)}, u32[]{:S(2)}) copy-start(s32[1024]{0:T(1024)} %param.17) | copy-start | bytes 12292
  165.0 381.7 %all-reduce.6.cloned.1.call-start = ((), (), s32[]{:S(2)}) async-start(), calls=%async_computation.2 | async-start | bytes 262144 | tf_op jit(solution)/shard_map/psum | solution.py:88
  459.6 7.1 %slice-start = ((s8[8388608]{0:T(1024)(128)(4,1)}), s8[4194304]{0:T(1024)(128)(4,1)S(1)}, s32[]{:S(2)}) async-start(s8[8388608]{0:T(1024)(128)(4,1)} %bitcast.69), calls=%async_computation.3 | async-start | bytes 8388608
  463.1 3.6 slice-start.1
  466.7 2.2 slice-start.2
  467.0 3.3 slice-start.3
  470.2 78.1 %copy-start.1 = (f32[3,32]{1,0:T(4,128)S(1)}, f32[3,32]{1,0:T(4,128)}, u32[]{:S(2)}) copy-start(f32[3,32]{1,0:T(4,128)} %param.11) | copy-start | bytes 1156
Sparse Core Ops, SparseCore 0:
  16.3 73.2 all-reduce.3
  165.2 123.5 all-gather.1
  478.3 68.4 all-reduce.5
where the time goes:
time: 558 us; the launch traced here: 555 us
  waiting for transfers between devices  236 us (42%)
  local copies, waits for them, and re-layouts  216 us (39%)
  other arithmetic  82.2 us (15%)
  between operations  14.8 us (3%)
    all_gather x1, waiting for transfers between devices, per_device(): everything = lax.all_gather(bottom, 'mode', axis=0, tiled=True)  109 us
    scatter x1, local copies, waits for them, and re-layouts, per_device(): bottom.at[:, :, rough_cells]  93.8 us
    psum x1, waiting for transfers between devices, per_device(): lax.psum(jnp.einsum('s,smzxy->zxy', weight_local, fresh), 'mode') / PAIRS  68.6 us
    psum x1, waiting for transfers between devices, per_device(): energy = lax.psum(partial_value, 'mode') / PAIRS  59 us
    sub x1, other arithmetic, per_device(): rhs = field + source[None] - speed * (along + across)  34.3 us
    all_gather x1, local copies, waits for them, and re-layouts, per_device(): everything = lax.all_gather(bottom, 'mode', axis=0, tiled=True)  23.2 us
    gather x3, local copies, waits for them, and re-layouts, per_device(): jnp.take_along_axis(values.transpose(2, 0, 1), targets[:, :, None], axis=1)  21.1 us
    gather x1, local copies, waits for them, and re-layouts, per_device(): values = everything[:, :, rough_cells]  19.9 us
  transfers between devices with their start and end apart: 5, of which 3 were waited for; matrix products, arithmetic and copies ran while one was open for 5% of the time, Pallas kernels for 0%

commit v1 on v0

--- a/solution.py
+++ b/solution.py
@@ -65,7 +65,15 @@
     bottom = down_new[:, :, 0].reshape(half, modes, rows * width)
     slots = rough_cells.shape[0]
     live = jnp.arange(slots, dtype=jnp.int32) < rough_count[0]
-    everything = lax.all_gather(bottom, "mode", axis=0, tiled=True)
+    ways, here = (lax.axis_size("mode"), lax.axis_index("mode"))
+    grown, reach = (bottom, 1)
+    while reach < ways:
+        theirs = lax.ppermute(grown, "mode", [(d, d ^ reach) for d in range(ways)])
+        mine_first = jnp.concatenate([grown, theirs], axis=0)
+        theirs_first = jnp.concatenate([theirs, grown], axis=0)
+        grown = jnp.where(here & reach == 0, mine_first, theirs_first)
+        reach = 2 * reach
+    everything = grown
     values = everything[:, :, rough_cells]
     targets = lax.dynamic_slice_in_dim(rough_map, position * half, half, 1)
     picked = jnp.take_along_axis(values.transpose(2, 0, 1), targets[:, :, None], axis=1).transpose(

time: 558 us -> 749 us (1.34)
  waiting for transfers between devices: 236 us -> 361 us
  other arithmetic: 82.2 us -> 123 us
  local copies, waits for them, and re-layouts: 216 us -> 239 us
    ppermute x0 -> x3, waiting for transfers between devices: none -> 232 us  [per_device(): theirs = lax.ppermute(grown, 'mode', [(d, d ^ reach) for d in range(ways)])]
    all_gather x1 -> x0, waiting for transfers between devices: 109 us -> none  [per_device(): everything = lax.all_gather(bottom, 'mode', axis=0, tiled=True)]
    concatenate x0 -> x2, local copies, waits for them, and re-layouts: none -> 46.5 us  [the longest x1 23.2 us: per_device(): mine_first = jnp.concatenate([grown, theirs], axis=0)]
    select_n x0 -> x3, other arithmetic: none -> 29.9 us  [per_device(): grown = jnp.where(here & reach == 0, mine_first, theirs_first)]
    all_gather x1 -> x0, local copies, waits for them, and re-layouts: 23.2 us -> none  [per_device(): everything = lax.all_gather(bottom, 'mode', axis=0, tiled=True)]
    concatenate x0 -> x1, other arithmetic: none -> 11 us  [per_device(): theirs_first = jnp.concatenate([theirs, grown], axis=0)]
  transfers between devices with their start and end apart: 5 -> 7, of which waited for: 3 -> 5; matrix products, arithmetic and copies ran while one was open for 5% -> 3% of each run, Pallas kernels for 0% -> 0%
where the time goes in v1:
time: 749 us; the launch traced here: 745 us
  waiting for transfers between devices  361 us (48%)
  local copies, waits for them, and re-layouts  239 us (32%)
  other arithmetic  123 us (16%)
  between operations  15.2 us (2%)
    ppermute x3, waiting for transfers between devices, per_device(): theirs = lax.ppermute(grown, 'mode', [(d, d ^ reach) for d in range(ways)])  232 us
    scatter x1, local copies, waits for them, and re-layouts, per_device(): bottom.at[:, :, rough_cells]  93.9 us
    psum x1, waiting for transfers between devices, per_device(): lax.psum(jnp.einsum('s,smzxy->zxy', weight_local, fresh), 'mode') / PAIRS  70 us
    psum x1, waiting for transfers between devices, per_device(): energy = lax.psum(partial_value, 'mode') / PAIRS  59.1 us
    sub x1, other arithmetic, per_device(): rhs = field + source[None] - speed * (along + across)  34.5 us
    select_n x3, other arithmetic, per_device(): grown = jnp.where(here & reach == 0, mine_first, theirs_first)  29.9 us
    concatenate x1, local copies, waits for them, and re-layouts, per_device(): mine_first = jnp.concatenate([grown, theirs], axis=0)  23.2 us
    concatenate x1, local copies, waits for them, and re-layouts, per_device(): theirs_first = jnp.concatenate([theirs, grown], axis=0)  23.2 us
  transfers between devices with their start and end apart: 7, of which 5 were waited for; matrix products, arithmetic and copies ran while one was open for 3% of the time, Pallas kernels for 0%

profile of v1, /device:TPU:0, one launch (start us, length us, event | category | flops | bytes accessed | tf_op | source)
XLA Modules:
  0.0 745.2 jit_solution(16352593027967324376)
XLA Ops:
  7.2 7.9 %bitcast_reduce_fusion = bf16[4,8,16,256]{3,2,1,0:T(8,128)(2,1)S(1)} fusion(f32[128,8,16,256]{3,2,1,0:T(8,128)} %param.10), kind=kLoop, calls=%fused_computation.101 | loop fusion | flops 4063232 | bytes 17039360 | tf_op jit(solution)/shard_map/s,smzxy->zxy/reduce_sum | solution.py:38
  15.2 0.4 fusion.23
  15.5 0.7 copy.283
  16.3 8.0 %fusion.37 = (f32[4,32,8,1,256]{4,3,2,1,0:T(1,128)S(1)}, f32[4,32,8,1,256]{4,3,2,1,0:T(1,128)S(1)}) fusion(f32[4,32,8,16,256]{4,3,2,1,0:T(8,128)} %bitcast.67), kind=kLoop, calls=%fused_computation.104 | loop fusion | bytes 4194304 | tf_op jit(solution)/shard_map/slice | solution.py:15
  24.4 2.5 collective-permute-start
  26.9 1.0 copy.254
  27.9 1.3 collective-permute-start.1
  29.4 0.9 broadcast_multiply_fusion.3
  30.5 59.1 %all-reduce.4.cloned.1.call-done = f32[8,16,256]{2,1,0:T(8,128)} async-done(((f32[8,16,256]{2,1,0:T(8,128)}), f32[8,16,256]{2,1,0:T(8,128)}) %all-reduce.4.cloned.1.call-update) | async-done | bytes 131088 | tf_op jit(solution)/shard_map/psum | solution.py:39
  89.6 0.9 add_divide_fusion.8
  90.5 0.6 broadcast_multiply_fusion.1
  91.2 1.1 copy.253
  92.3 2.3 copy.255
  94.6 34.5 %fusion.5 = f32[4,32,8,16,256]{4,3,2,1,0:T(8,128)} fusion(f32[4,32,8,16,256]{4,3,2,1,0:T(8,128)} %bitcast.68, f32[4,32,8,1,256]{4,3,2,1,0:T(1,128)S(1)} %copy.255, f32[4,32,8,1,256]{4,3,2,1,0:T(1,128)S(1)} %copy.253, f32[4]{0:T(128)S(1)} %get-tuple-element.33, f32[4]{0:T(128)S(1)} %get-tuple-element.35, f32[4]{0:T(128)S(1)} %get-tuple-element.32, ...), kind=kLoop, calls=%fused_computation.11 | loop fusion | flops 67108864 | bytes 39846080 | tf_op jit(solution)/shard_map/sub | solution.py:53
  129.0 9.2 %fusion.36 = (f32[2,32,8,16,256]{4,3,2,1,0:T(8,128)}, f32[2,32,8,16,256]{4,3,2,1,0:T(8,128)S(1)}) fusion(f32[4,32,8,16,256]{4,3,2,1,0:T(8,128)} %fusion.5), kind=kLoop, calls=%fused_computation.103 | loop fusion | bytes 33554432 | tf_op jit(solution)/shard_map/slice | solution.py:87
  138.3 1.1 divide_dynamic-update-slice_fusion
  139.3 0.2 constant_dynamic-update-slice_fusion.12
  140.3 3.0 fusion.38
  143.3 3.4 copy-done.2
  146.7 2.5 squeeze.36
  149.2 2.4 squeeze.37
  151.6 2.4 squeeze.38
  154.0 2.4 squeeze.39
  156.4 2.4 squeeze.40
  158.7 1.2 squeeze.41
  159.9 1.2 squeeze.42
  161.3 4.1 add_divide_fusion.7
  165.4 0.7 collective-permute-start.2
  166.1 22.5 %collective-permute-done.2 = f32[2,32,4096]{2,1,0:T(8,128)} collective-permute-done((f32[2,32,4096]{2,1,0:T(8,128)S(1)}, f32[2,32,4096]{2,1,0:T(8,128)}, u32[]{:S(2)}, u32[]{:S(2)}) %collective-permute-start.2) | collective-permute-done | bytes 1048608 | tf_op jit(solution)/shard_map/ppermute | solution.py:71
  188.6 1.8 maximum_select_fusion.1
  190.5 0.7 collective-permute-start.3
  191.2 44.1 %collective-permute-done.3 = f32[4,32,4096]{2,1,0:T(8,128)} collective-permute-done((f32[4,32,4096]{2,1,0:T(8,128)S(1)}, f32[4,32,4096]{2,1,0:T(8,128)}, u32[]{:S(2)}, u32[]{:S(2)}) %collective-permute-start.3) | collective-permute-done | bytes 2097184 | tf_op jit(solution)/shard_map/ppermute | solution.py:71
  235.3 4.8 maximum_select_fusion
  240.1 1.3 collective-permute-start.4
  241.4 0.8 bitcast_or_fusion
  242.5 0.3 reshape.137
  242.7 0.8 and_bitcast_fusion
  243.5 0.3 copy.256
  244.5 4.4 copy.261
  248.9 5.7 gather_fusion.1
  254.6 165.0 %collective-permute-done.4 = f32[8,32,4096]{2,1,0:T(8,128)} collective-permute-done((f32[8,32,4096]{2,1,0:T(8,128)}, f32[8,32,4096]{2,1,0:T(8,128)}, u32[]{:S(2)}, u32[]{:S(2)}) %collective-permute-start.4) | collective-permute-done | bytes 4194336 | tf_op jit(solution)/shard_map/ppermute | solution.py:71
  419.6 11.0 %pad_maximum_fusion.4 = (f32[16,32,4096]{2,1,0:T(8,128)}, f32[16,32,4096]{2,1,0:T(8,128)}) fusion(f32[8,32,4096]{2,1,0:T(8,128)} %maximum_select_fusion, f32[8,32,4096]{2,1,0:T(8,128)} %collective-permute-done.4), kind=kLoop, calls=%fused_computation.24 | loop fusion | flops 4194304 | bytes 25165824 | tf_op jit(solution)/shard_map/concatenate | solution.py:73
  430.7 23.2 %copy.257 = f32[16,32,4096]{1,0,2:T(8,128)} copy(f32[16,32,4096]{2,1,0:T(8,128)} %get-tuple-element.19) | data formatting | bytes 16777216 | tf_op jit(solution)/shard_map/concatenate | solution.py:72
  453.9 23.2 %copy.258 = f32[16,32,4096]{1,0,2:T(8,128)} copy(f32[16,32,4096]{2,1,0:T(8,128)} %get-tuple-element.18) | data formatting | bytes 16777216 | tf_op jit(solution)/shard_map/concatenate | solution.py:73
  477.1 23.3 %broadcast_select_fusion = f32[16,32,4096]{1,0,2:T(8,128)} fusion(f32[16,32,4096]{1,0,2:T(8,128)} %copy.257, f32[16,32,4096]{1,0,2:T(8,128)} %copy.258, pred[]{:T(512)S(6)} %eq.9), kind=kLoop, calls=%fused_computation.22 | loop fusion | flops 2097152 | bytes 25165824 | tf_op jit(solution)/shard_map/jit(_where)/select_n | solution.py:74
  500.4 20.1 %gather_fusion = f32[1024,16,32]{2,1,0:T(8,128)} fusion(f32[16,32,4096]{1,0,2:T(8,128)} %broadcast_select_fusion, s32[1024]{0:T(1024)S(1)} %get-tuple-element.29), kind=kCustom, calls=%fused_computation | custom fusion | bytes 4198400 | tf_op jit(solution)/shard_map/gather | solution.py:77
  520.5 20.5 %gather_fusion.2 = f32[2048,32]{1,0:T(8,128)S(1)} fusion(f32[1024,16,32]{2,1,0:T(8,128)} %gather_fusion, s32[2048]{0:T(1024)S(1)} %reshape.137), kind=kCustom, calls=%fused_computation.2 | custom fusion | bytes 540672 | tf_op jit(solution)/shard_map/jit(take_along_axis)/gather | solution.py:79
  541.0 3.9 fusion.22
  544.9 93.9 %scatter_fusion = f32[2,32,4096]{1,0,2:T(2,128)} fusion(f32[2,32,4096]{1,0,2:T(2,128)} %copy.261, s32[1024]{0:T(1024)S(1)} %get-tuple-element.30, f32[1024,2,32]{2,1,0:T(2,128)S(1)} %fusion.22), kind=kCustom, calls=%fused_computation.3 | custom fusion | bytes 790528 | tf_op jit(solution)/shard_map/scatter | solution.py:83
  638.8 5.8 broadcast_multiply_fusion
  644.6 3.6 copy.271
  648.2 1.6 constant_dynamic-update-slice_fusion.6
  649.9 1.9 constant_dynamic-update-slice_fusion.5
  651.8 1.6 constant_dynamic-update-slice_fusion.4
  653.4 1.9 constant_dynamic-update-slice_fusion.3
  655.6 0.3 constant_dynamic-update-slice_fusion.1
  656.1 0.3 fusion.14
  656.4 1.1 slice-done.2
  657.5 1.3 slice-done.3
  658.9 6.9 fusion.32
  665.7 0.4 fusion.25
  666.1 0.7 copy.282
  666.8 70.0 %all-reduce.6.cloned.1.call-done = f32[8,16,256]{2,1,0:T(8,128)} async-done(((f32[8,16,256]{2,1,0:T(8,128)}), f32[8,16,256]{2,1,0:T(8,128)}) %all-reduce.6.cloned.1.call-update) | async-done | bytes 131088 | tf_op jit(solution)/shard_map/psum | solution.py:96
  736.8 1.6 broadcast_multiply_fusion.4
  (54 shorter events, 2.1 us)
Async XLA Ops:
  7.2 22.0 %copy-start = (f32[3,32]{1,0:T(4,128)S(1)}, f32[3,32]{1,0:T(4,128)}, u32[]{:S(2)}) copy-start(f32[3,32]{1,0:T(4,128)} %param.11) | copy-start | bytes 1156
  7.2 82.4 %all-reduce.4.cloned.1.call-start = ((), (), s32[]{:S(2)}) async-start(), calls=%async_computation | async-start | bytes 262144 | tf_op jit(solution)/shard_map/psum | solution.py:39
  7.2 7.9 %copy-start.9 = (f32[32]{0:T(128)S(1)}, f32[32]{0:T(128)}, u32[]{:S(2)}) copy-start(f32[32]{0:T(128)} %param.15) | copy-start | bytes 388
  15.1 14.2 %copy-start.4 = (f32[16,256]{1,0:T(8,128)S(1)}, f32[16,256]{1,0:T(8,128)}, u32[]{:S(2)}) copy-start(f32[16,256]{1,0:T(8,128)} %param.16) | copy-start | bytes 49156
  15.1 14.2 %copy-start.7 = (f32[32]{0:T(128)S(1)}, f32[32]{0:T(128)}, u32[]{:S(2)}) copy-start(f32[32]{0:T(128)} %param.12) | copy-start | bytes 388
  15.1 14.2 %copy-start.5 = (f32[32]{0:T(128)S(1)}, f32[32]{0:T(128)}, u32[]{:S(2)}) copy-start(f32[32]{0:T(128)} %param.14) | copy-start | bytes 388
  15.1 15.2 %copy-start.8 = (f32[32]{0:T(128)S(1)}, f32[32]{0:T(128)}, u32[]{:S(2)}) copy-start(f32[32]{0:T(128)} %param.13) | copy-start | bytes 388
  16.2 720.6 %all-reduce.6.cloned.1.call-start = ((), (), s32[]{:S(2)}) async-start(), calls=%async_computation.1 | async-start | bytes 262144 | tf_op jit(solution)/shard_map/psum | solution.py:96
  24.4 66.8 %collective-permute-start = (f32[4,32,8,1,256]{4,2,3,1,0:T(8,128)S(1)}, f32[4,32,8,1,256]{4,2,3,1,0:T(8,128)S(1)}, u32[]{:S(2)}, u32[]{:S(2)}) collective-permute-start(f32[4,32,8,1,256]{4,2,3,1,0:T(8,128)S(1)} %copy.252), channel_id=1, source_target_pairs={{0,8},{8,16},{16,24},{1,9},{9,17},{17,25},{2,10},{10,18},{18,26},{... | collective-permute-start | bytes 3145736 | tf_op jit(solution)/shard_map/ppermute | solution.py:14
  27.9 64.4 %collective-permute-start.1 = (f32[4,32,8,1,256]{4,2,3,1,0:T(8,128)}, f32[4,32,8,1,256]{4,2,3,1,0:T(8,128)}, u32[]{:S(2)}, u32[]{:S(2)}) collective-permute-start(f32[4,32,8,1,256]{4,2,3,1,0:T(8,128)} %copy.254), channel_id=1, source_target_pairs={{8,0},{16,8},{24,16},{9,1},{17,9},{25,17},{10,2},{18,10},{26,18},{... | collective-permute-start | bytes 3145736 | tf_op jit(solution)/shard_map/ppermute | solution.py:17
  143.3 3.4 copy-start.2
  146.7 12.1 %copy-start.3 = (f32[2,32,1,16,256]{4,3,2,1,0:T(8,128)S(1)}, f32[2,32,1,16,256]{4,3,2,1,0:T(8,128)}, u32[]{:S(2)}) copy-start(f32[2,32,1,16,256]{4,3,2,1,0:T(8,128)} %get-tuple-element.23) | copy-start | bytes 3145732
  165.4 79.0 %copy-start.6 = (s32[1024]{0:T(1024)S(1)}, s32[1024]{0:T(1024)}, u32[]{:S(2)}) copy-start(s32[1024]{0:T(1024)} %param.17) | copy-start | bytes 12292
  165.4 23.2 %collective-permute-start.2 = (f32[2,32,4096]{2,1,0:T(8,128)S(1)}, f32[2,32,4096]{2,1,0:T(8,128)}, u32[]{:S(2)}, u32[]{:S(2)}) collective-permute-start(f32[2,32,4096]{2,1,0:T(8,128)S(1)} %add_divide_fusion.7), channel_id=1, source_target_pairs={{0,1},{1,0},{2,3},{3,2},{4,5},{5,4},{6,7},{7,6},{8,9},{9,8},{10,11... | collective-permute-start | bytes 3145736 | tf_op jit(solution)/shard_map/ppermute | solution.py:71
  190.5 44.8 %collective-permute-start.3 = (f32[4,32,4096]{2,1,0:T(8,128)S(1)}, f32[4,32,4096]{2,1,0:T(8,128)}, u32[]{:S(2)}, u32[]{:S(2)}) collective-permute-start(f32[4,32,4096]{2,1,0:T(8,128)S(1)} %maximum_select_fusion.1), channel_id=1, source_target_pairs={{0,2},{1,3},{2,0},{3,1},{4,6},{5,7},{6,4},{7,5},{8,10},{9,11},{10,... | collective-permute-start | bytes 6291464 | tf_op jit(solution)/shard_map/ppermute | solution.py:71
  240.1 179.5 %collective-permute-start.4 = (f32[8,32,4096]{2,1,0:T(8,128)}, f32[8,32,4096]{2,1,0:T(8,128)}, u32[]{:S(2)}, u32[]{:S(2)}) collective-permute-start(f32[8,32,4096]{2,1,0:T(8,128)} %maximum_select_fusion), channel_id=1, source_target_pairs={{0,4},{1,5},{2,6},{3,7},{4,0},{5,1},{6,2},{7,3},{8,12},{9,13},{10,... | collective-permute-start | bytes 12582920 | tf_op jit(solution)/shard_map/ppermute | solution.py:71
  648.2 7.1 slice-start
  651.8 3.6 slice-start.1
  655.3 2.2 slice-start.2
  655.6 3.3 slice-start.3
  658.9 79.5 %copy-start.1 = (f32[3,32]{1,0:T(4,128)S(1)}, f32[3,32]{1,0:T(4,128)}, u32[]{:S(2)}) copy-start(f32[3,32]{1,0:T(4,128)} %param.11) | copy-start | bytes 1156
Sparse Core Ops, SparseCore 0:
  16.3 73.2 all-reduce.3
  666.9 69.8 all-reduce.5
